TPU v7x, 32 devices: a whole 2x2x4 slice. The times are simulated.
32 devices in a mesh: cfg: 2 (over y), space: 8 (over z, x), tm: 2 (over core).
Axes of the slice: x: 2, y: 2, z: 4, core: 2. Of those that a mesh axis runs over, the one named last changes fastest.
Arguments:
- eigvecs: bfloat16 [4, 2, 3, 1536, 256], P(('cfg', 'tm'), None, None, 'space'), parts along dimension 0, may hold values from -6 to 6
- momenta: int32 [3, 3], replicated, may hold values from -2 to 2, as said below
- pair_list: int32 [8, 2], P('tm'), may hold values from 0 to 1
- panels: bfloat16 [16, 2, 1024, 1024], P(('cfg', 'tm'), None, 'space'), parts along dimension 0, may hold values from -6 to 6
Outputs:
- dressed: bfloat16 [16, 3, 2, 1024, 1024], P(('cfg', 'tm'), None, None, 'space'), parts along dimension 0
There are 2 independent parts, one for each index of `cfg`. A program takes and returns all parts, laid end to end along the dimension named above; an argument that names none is the same for every part. Nothing has to cross between parts.
Inputs may be any that keep to these rules, and one draw needn't show every extreme that they name: `momenta`: the first component of every momentum is nonzero.
All inputs are finite; a program needn't handle non-finite values.
Results may differ from a plain program's by a relative error of at most 0.0075.
Values may be sent and summed in bfloat16 or wider, within the bound.
A program may use at most 64 MiB of HBM per device.

v0:
```python
import math
import jax
import jax.numpy as jnp
from jax import lax
from jax.sharding import PartitionSpec as P

LX = 64


def phased_block(cosine, sine_part, real_part, imag_part):
    cos_col = cosine[:, None]
    sin_col = sine_part[:, None]
    wave_re = cos_col * real_part + sin_col * imag_part
    wave_im = cos_col * imag_part - sin_col * real_part
    upper = jnp.concatenate([wave_re, wave_im], -1)
    lower = jnp.concatenate([wave_im, -wave_re], -1)
    return jnp.stack([upper, lower], -4).astype(jnp.bfloat16)


def local(eigvecs, momenta, pair_list, panels):
    slice_count, _, colors, slab_sites, vectors = eigvecs.shape
    mom_count = momenta.shape[0]
    space_count = lax.axis_size("space")
    first_site = lax.axis_index("space") * slab_sites
    site_index = first_site + jnp.arange(slab_sites, dtype=jnp.int32)
    xpos = site_index % LX
    ypos = site_index // LX % LX
    zpos = site_index // (LX * LX)
    wave = (
        momenta[:, 0:1] * xpos[None, :]
        + momenta[:, 1:2] * ypos[None, :]
        + momenta[:, 2:3] * zpos[None, :]
    )
    wave = jnp.mod(wave, LX)
    angle = wave.astype(jnp.float32) * jnp.float32(2.0 * math.pi / LX)
    cosine = jnp.cos(angle)
    sine_part = jnp.sin(angle)
    factor = 1.0 / math.sqrt(6.0 * slab_sites * space_count * vectors)
    real_part = eigvecs[:, 0].astype(jnp.float32)
    imag_part = eigvecs[:, 1].astype(jnp.float32)
    phased_all = jnp.concatenate(
        [
            phased_block(cosine[moment], sine_part[moment], real_part, imag_part)
            for moment in range(mom_count)
        ],
        -1,
    )
    phased_all = phased_all.reshape(slice_count, 2, colors, slab_sites, mom_count, 2 * vectors)
    gram_local = jnp.einsum(
        "trcsk,trcsml->tmkl", eigvecs, phased_all, preferred_element_type=jnp.float32
    )
    gram_local = factor * gram_local
    summed = lax.psum(gram_local, "space")
    own_fields = summed.astype(jnp.bfloat16)
    meson_fields = lax.all_gather(own_fields, "tm", axis=0, tiled=True)
    pair_count = pair_list.shape[0]
    panel_rows = panels.shape[2]
    panel_width = panels.shape[3]
    spins = panel_width // vectors
    source_fields = jnp.take(meson_fields, pair_list[:, 0], axis=0).reshape(
        pair_count, mom_count, vectors, 2, vectors
    )
    sink_fields = jnp.take(meson_fields, pair_list[:, 1], axis=0).reshape(
        pair_count, mom_count, vectors, 2, vectors
    )
    panel_parts = panels.reshape(pair_count, 2, panel_rows, spins, vectors)
    panel_re = panel_parts[:, 0]
    panel_im = panel_parts[:, 1]
    panel_mix = jnp.stack(
        [jnp.stack([panel_re, panel_im], 1), jnp.stack([panel_im, -panel_re], 1)], 1
    )
    right_dressed = jnp.einsum(
        "porxbk,pmlrk->pmoxbl", panel_mix, source_fields, preferred_element_type=jnp.float32
    )
    right_dressed = right_dressed.astype(jnp.bfloat16).reshape(
        pair_count * mom_count, 2, panel_rows, panel_width
    )
    turned = lax.all_to_all(right_dressed, "space", split_axis=3, concat_axis=2, tiled=True)
    column_count = turned.shape[3]
    turned = turned.reshape(pair_count, mom_count, 2, spins, vectors, column_count)
    turned_re = turned[:, :, 0]
    turned_im = turned[:, :, 1]
    mixed_parts = jnp.stack(
        [jnp.stack([turned_re, -turned_im], 2), jnp.stack([turned_im, turned_re], 2)], 2
    )
    dressed = jnp.einsum(
        "pmorajc,pmkrj->pmocak", mixed_parts, sink_fields, preferred_element_type=jnp.float32
    )
    return dressed.reshape(pair_count, mom_count, 2, column_count, panel_width).astype(jnp.bfloat16)


def solution(mesh):
    placed = (
        P(("cfg", "tm"), None, None, "space", None),
        P(),
        P("tm", None),
        P(("cfg", "tm"), None, "space", None),
    )
    return jax.shard_map(
        local,
        mesh=mesh,
        in_specs=placed,
        out_specs=P(("cfg", "tm"), None, None, "space", None),
        check_vma=False,
    )
```

profile of v0, /device:TPU:0, one launch (start us, length us, event | category | flops | bytes accessed | tf_op | source)
XLA Modules:
  0.0 343.8 jit_solution(5193341892418195743)
XLA Ops:
  6.5 0.0 all-gather.2.cloned.1.call-start
  6.6 1.0 slice_reduce_fusion.2
  7.6 0.1 fusion.37
  7.7 0.0 copy-start.3
  7.8 1.6 fusion.30
  9.3 0.1 maximum_bitcast_fusion.9
  9.4 0.1 pad_maximum_fusion
  9.5 0.0 copy-done.3
  9.6 0.3 fusion.28
  9.8 0.1 maximum_bitcast_fusion.11
  10.0 0.1 maximum_bitcast_fusion.13
  10.1 1.2 fusion.17
  11.3 83.3 %all-reduce.1 = bf16[1,3,256,512]{2,3,1,0:T(8,128)(2,1)S(1)} all-reduce(f32[1,3,256,512]{2,3,1,0:T(8,128)S(1)} %fusion.17), channel_id=1, replica_groups=mesh['cfg'=2,'space'=8,'tm'=2] {'space'}, use_global_device_ids=true, to_apply=%region_0.1 | all-reduce | flops 393216 | bytes 2359296 | tf_op jit(solution)/shard_map/psum | solution.py:53
  94.7 1.3 copy.48
  95.9 0.0 all-gather.2.cloned.1.call-update
  95.9 3.0 copy.49
  99.0 1.5 fusion.42
  100.4 1.5 copy.77
  102.0 1.2 neg.44
  103.2 0.0 copy-start.4
  103.2 0.0 copy-start.2
  103.2 2.4 copy.76
  105.6 2.3 copy.53
  107.9 0.0 copy-done.4
  107.9 0.0 copy-done.2
  107.9 2.7 maximum_bitcast_fusion.6
  110.7 0.0 all-gather.2.cloned.1.call-done
  110.7 2.2 gather_fusion.1
  112.8 2.0 broadcast_select_fusion
  114.9 3.8 %reshape.415 = bf16[4,3,256,2,256]{4,3,2,1,0:T(2,128)(2,1)S(1)} reshape(bf16[4,3,256,512]{3,2,1,0:T(8,128)(2,1)} %broadcast_select_fusion) | data formatting | bytes 6291456 | tf_op jit(solution)/shard_map/reshape | solution.py:60
  118.6 6.2 %bitcast_convert_fusion.1 = bf16[4,3,256,2,128,4]{4,2,5,3,1,0:T(8,128)(2,1)S(1)} fusion(bf16[4,1,2,128,4,256]{5,3,2,4,1,0:T(8,128)(2,1)} %maximum_bitcast_fusion.6, bf16[4,1,2,128,4,256]{5,3,2,4,1,0:T(8,128)(2,1)} %copy.53, bf16[4,3,256,2,256,1,1]{4,3,2,1,0,6,5:T(2,128)(2,1)S(1)} %bitcast.120), kind=kOutput, calls=%fused_computation.7 | convolution fusion | flops 3232759808 | bytes 13631488 | tf_op jit(solution)/shard_map/porxbk,pmlrk->pmoxbl/dot_general | solution.py:72
  124.8 36.6 %copy.55 = bf16[12,2,128,1024]{2,1,0,3:T(2,128)(2,1)} copy(bf16[12,2,128,1024]{2,3,1,0:T(8,128)(2,1)S(1)} %bitcast.117) | data formatting | bytes 12582912 | tf_op jit(solution)/shard_map/reshape | solution.py:75
  161.5 0.0 copy-start.1
  161.5 5.1 %all-to-all-start = ((bf16[12,2,128,1024]{2,1,0,3:T(2,128)(2,1)}), bf16[12,2,128,1024]{2,1,0,3:T(2,128)(2,1)}, u32[]{:S(2)}, u32[]{:S(2)}) async-start(bf16[12,2,128,1024]{2,1,0,3:T(2,128)(2,1)} %copy.55), calls=%async_computation | async-start | bytes 12582912 | tf_op jit(solution)/shard_map/all_to_all | solution.py:78
  166.5 0.0 copy-done.1
  166.6 2.5 gather_fusion
  169.0 2.3 broadcast_select_fusion.1
  171.3 3.1 reshape.414
  174.3 125.2 %all-to-all-done = bf16[12,2,128,1024]{2,1,0,3:T(2,128)(2,1)} async-done(((bf16[12,2,128,1024]{2,1,0,3:T(2,128)(2,1)}), bf16[12,2,128,1024]{2,1,0,3:T(2,128)(2,1)}, u32[]{:S(2)}, u32[]{:S(2)}) %all-to-all-start) | async-done | bytes 6291488 | tf_op jit(solution)/shard_map/all_to_all | solution.py:78
  299.6 6.9 %copy.56 = bf16[12,2,128,1024]{2,3,1,0:T(8,128)(2,1)} copy(bf16[12,2,128,1024]{2,1,0,3:T(2,128)(2,1)} %all-to-all-done) | data formatting | bytes 12582912 | tf_op jit(solution)/shard_map/all_to_all | solution.py:78
  306.4 8.6 %copy.57 = bf16[12,2,8,128,128]{4,3,2,1,0:T(8,128)(2,1)} copy(bf16[12,2,8,128,128]{3,4,2,1,0:T(8,128)(2,1)} %bitcast.114) | data formatting | bytes 12582912 | tf_op jit(solution)/shard_map/all_to_all | solution.py:78
  315.1 0.0 copy-start
  315.1 3.4 slice_bitcast_fusion
  318.5 1.2 copy-done
  319.7 0.4 fusion.41
  320.1 1.0 maximum_bitcast_fusion
  321.1 7.2 %bitcast_convert_fusion = bf16[4,3,256,2,4,128]{5,2,4,3,1,0:T(8,128)(2,1)} fusion(bf16[4,3,1,2,4,256,128]{6,5,3,4,2,1,0:T(8,128)(2,1)S(1)} %get-tuple-element.16, bf16[4,3,1,2,4,256,128]{6,5,3,4,2,1,0:T(8,128)(2,1)S(1)} %get-tuple-element.15, bf16[4,3,256,2,256,1,1]{4,3,2,1,0,6,5:T(2,128)(2,1)} %bitcast.119), kind=kOutput, calls=%fused_computation.6 | convolution fusion | flops 3249537024 | bytes 22020096 | tf_op jit(solution)/shard_map/pmorajc,pmkrj->pmocak/dot_general | solution.py:86
  328.3 8.6 %copy.62 = bf16[4,3,2,128,1024]{4,3,2,1,0:T(8,128)(2,1)} copy(bf16[4,3,2,128,1024]{3,4,2,1,0:T(8,128)(2,1)} %bitcast.118) | data formatting | bytes 12582912 | tf_op jit(solution)/shard_map/convert_element_type | solution.py:89
  (6 shorter events, 0.1 us)
Async XLA Ops:
  6.5 104.1 %all-gather.2.cloned.1.call-start = ((), (), s32[]{:S(2)}) async-start(), calls=%async_computation.1 | async-start | bytes 2359296 | tf_op jit(solution)/shard_map/all_gather | solution.py:55
  7.7 1.8 copy-start.3
  103.2 4.7 %copy-start.4 = (s32[4,2]{0,1:T(2,128)S(1)}, s32[4,2]{0,1:T(2,128)}, u32[]{:S(2)}) copy-start(s32[4,2]{0,1:T(2,128)} %param.8) | copy-start | bytes 100
  103.2 4.7 %copy-start.2 = (bf16[4,1,128,4,256]{4,2,1,3,0:T(8,128)(2,1)S(1)}, bf16[4,1,128,4,256]{4,2,1,3,0:T(8,128)(2,1)}, u32[]{:S(2)}) copy-start(bf16[4,1,128,4,256]{4,2,1,3,0:T(8,128)(2,1)} %neg.44) | copy-start | bytes 3145732
  161.5 5.1 %copy-start.1 = (bf16[2,3,256,512]{3,2,1,0:T(8,128)(2,1)S(1)}, bf16[2,3,256,512]{3,2,1,0:T(8,128)(2,1)}, u32[]{:S(2)}) copy-start(bf16[2,3,256,512]{3,2,1,0:T(8,128)(2,1)} %all-gather.2.cloned.1.call-done) | copy-start | bytes 4718596
  161.5 138.1 %all-to-all-start = ((bf16[12,2,128,1024]{2,1,0,3:T(2,128)(2,1)}), bf16[12,2,128,1024]{2,1,0,3:T(2,128)(2,1)}, u32[]{:S(2)}, u32[]{:S(2)}) async-start(bf16[12,2,128,1024]{2,1,0,3:T(2,128)(2,1)} %copy.55), calls=%async_computation | async-start | bytes 12582912 | tf_op jit(solution)/shard_map/all_to_all | solution.py:78
  315.1 4.6 %copy-start = (bf16[12,2,8,128,128]{4,3,2,1,0:T(8,128)(2,1)S(1)}, bf16[12,2,8,128,128]{4,3,2,1,0:T(8,128)(2,1)}, u32[]{:S(2)}) copy-start(bf16[12,2,8,128,128]{4,3,2,1,0:T(8,128)(2,1)} %copy.57) | copy-start | bytes 18874372
Sparse Core Ops, SparseCore 0:
  96.1 7.9 all-gather.1
where the time goes:
time: 345 us; the launch traced here: 344 us
  waiting for transfers between devices  125 us (36%)
  local copies, waits for them, and re-layouts  89.8 us (26%)
  blocking collectives  83.3 us (24%)
  matrix products  14.6 us (4%)
  between operations  13.6 us (4%)
  other arithmetic  12 us (3%)
  starting transfers between devices  5.08 us (1%)
    all_to_all x1, waiting for transfers between devices, local(): lax.all_to_all(right_dressed, 'space', split_axis=3, concat_axis=2, tiled...  125 us
    psum x1, blocking collectives, local(): summed = lax.psum(gram_local, 'space')  83.3 us
    reshape x1, local copies, waits for them, and re-layouts, local(): right_dressed.astype(jnp.bfloat16)  36.6 us
    all_to_all x2, local copies, waits for them, and re-layouts, local(): lax.all_to_all(right_dressed, 'space', split_axis=3, concat_axis=2, tiled...  15.5 us
    unnamed x14, local copies, waits for them, and re-layouts  11.6 us
    convert_element_type x1, local copies, waits for them, and re-layouts, local(): dressed.reshape(pair_count, mom_count, 2, column_count, panel_width)  8.62 us
    dot_general x1, matrix products, local(): jnp.einsum('pmorajc,pmkrj->pmocak', mixed_parts, sink_fields, preferred_e...  7.2 us
  transfers between devices with their start and end apart: 2, of which 1 were waited for; matrix products, arithmetic and copies ran while one was open for 7% of the time, Pallas kernels for 0%

commit v1 on v0

--- a/solution.py
+++ b/solution.py
@@ -75,7 +75,9 @@
     right_dressed = right_dressed.astype(jnp.bfloat16).reshape(
         pair_count * mom_count, 2, panel_rows, panel_width
     )
-    turned = lax.all_to_all(right_dressed, "space", split_axis=3, concat_axis=2, tiled=True)
+    pieces = jnp.split(right_dressed, lax.axis_size("space"), axis=3)
+    received = lax.all_to_all(jnp.stack(pieces), "space", 0, 0)
+    turned = jnp.concatenate(received, axis=2)
     column_count = turned.shape[3]
     turned = turned.reshape(pair_count, mom_count, 2, spins, vectors, column_count)
     turned_re = turned[:, :, 0]

time: 345 us -> 317 us (0.919)
  local copies, waits for them, and re-layouts: 89.8 us -> 64.3 us
    reshape x1 -> x0, local copies, waits for them, and re-layouts: 36.6 us -> none  [local(): right_dressed.astype(jnp.bfloat16)]
    unnamed x14 -> x33, local copies, waits for them, and re-layouts: 11.6 us -> 30 us
    all_to_all x2 -> x1, local copies, waits for them, and re-layouts: 15.5 us -> 4.14 us  [local(): received = lax.all_to_all(jnp.stack(pieces), 'space', 0, 0)]
where the time goes in v1:
time: 317 us; the launch traced here: 316 us
  waiting for transfers between devices  125 us (39%)
  blocking collectives  83.3 us (26%)
  local copies, waits for them, and re-layouts  64.3 us (20%)
  between operations  13.7 us (4%)
  matrix products  12.8 us (4%)
  other arithmetic  12.1 us (4%)
  starting transfers between devices  5.08 us (2%)
    all_to_all x1, waiting for transfers between devices, local(): received = lax.all_to_all(jnp.stack(pieces), 'space', 0, 0)  125 us
    psum x1, blocking collectives, local(): summed = lax.psum(gram_local, 'space')  83.3 us
    unnamed x33, local copies, waits for them, and re-layouts  30 us
    convert_element_type x1, local copies, waits for them, and re-layouts, local(): dressed.reshape(pair_count, mom_count, 2, column_count, panel_width)  8.62 us
  transfers between devices with their start and end apart: 2, of which 1 were waited for; matrix products, arithmetic and copies ran while one was open for 7% of the time, Pallas kernels for 0%

profile of v1, /device:TPU:0, one launch (start us, length us, event | category | flops | bytes accessed | tf_op | source)
XLA Modules:
  0.0 316.4 jit_solution(9828272889111505163)
XLA Ops:
  6.6 1.0 slice_reduce_fusion.2
  7.6 0.1 fusion.37
  7.8 1.6 fusion.30
  9.4 0.1 pad_maximum_fusion
  9.6 0.3 fusion.28
  10.1 1.2 fusion.17
  11.3 83.3 %all-reduce.1 = bf16[1,3,256,512]{2,3,1,0:T(8,128)(2,1)S(1)} all-reduce(f32[1,3,256,512]{2,3,1,0:T(8,128)S(1)} %fusion.17), channel_id=1, replica_groups=mesh['cfg'=2,'space'=8,'tm'=2] {'space'}, use_global_device_ids=true, to_apply=%region_0.1 | all-reduce | flops 393216 | bytes 2359296 | tf_op jit(solution)/shard_map/psum | solution.py:53
  94.7 1.2 copy.40
  95.9 3.0 copy.41
  99.0 1.5 fusion.43
  100.4 1.5 copy.75
  101.9 1.2 neg.44
  103.2 2.4 copy.74
  105.5 2.4 copy.45
  107.9 2.8 maximum_bitcast_fusion.6
  110.7 2.2 gather_fusion.1
  112.9 2.0 broadcast_select_fusion
  114.9 3.8 %reshape.414 = bf16[4,3,256,2,256]{4,3,2,1,0:T(2,128)(2,1)S(1)} reshape(bf16[4,3,256,512]{3,2,1,0:T(8,128)(2,1)} %broadcast_select_fusion) | data formatting | bytes 6291456 | tf_op jit(solution)/shard_map/reshape | solution.py:60
  118.7 6.2 %bitcast_convert_fusion.1 = bf16[4,3,256,2,128,4]{4,2,5,3,1,0:T(8,128)(2,1)S(1)} fusion(bf16[4,1,2,128,4,256]{5,3,2,4,1,0:T(8,128)(2,1)} %maximum_bitcast_fusion.6, bf16[4,1,2,128,4,256]{5,3,2,4,1,0:T(8,128)(2,1)} %copy.45, bf16[4,3,256,2,256,1,1]{4,3,2,1,0,6,5:T(2,128)(2,1)S(1)} %bitcast.134), kind=kOutput, calls=%fused_computation.7 | convolution fusion | flops 3232759808 | bytes 13631488 | tf_op jit(solution)/shard_map/porxbk,pmlrk->pmoxbl/dot_general | solution.py:72
  124.9 3.1 fusion.42
  128.0 2.3 copy.76
  130.3 2.1 bitcast_dynamic-update-slice_fusion.7
  132.4 2.3 copy.77
  134.7 2.3 copy.78
  137.0 2.3 copy.79
  139.3 1.2 copy.80
  140.5 0.4 copy.81
  140.9 0.4 copy.82
  141.2 0.4 copy.83
  141.7 2.2 bitcast_dynamic-update-slice_fusion.6
  143.9 2.1 bitcast_dynamic-update-slice_fusion.5
  146.0 1.0 bitcast_dynamic-update-slice_fusion.4
  146.9 1.0 bitcast_dynamic-update-slice_fusion.3
  147.9 0.9 bitcast_dynamic-update-slice_fusion.2
  148.8 0.9 bitcast_dynamic-update-slice_fusion.1
  149.7 0.9 bitcast_dynamic-update-slice_fusion
  150.7 5.1 %all-to-all-start = ((bf16[8,12,2,128,128]{4,3,2,1,0:T(8,128)(2,1)}), bf16[8,12,2,128,128]{4,3,2,1,0:T(8,128)(2,1)}, u32[]{:S(2)}, u32[]{:S(2)}) async-start(bf16[8,12,2,128,128]{4,3,2,1,0:T(8,128)(2,1)} %bitcast_dynamic-update-slice_fusion), calls=%async_computation | async-start | bytes 12582912 | tf_op jit(solution)/shard_map/all_to_all | solution.py:79
  155.8 2.5 gather_fusion
  158.2 2.3 broadcast_select_fusion.1
  160.5 3.1 reshape.413
  163.5 125.2 %all-to-all-done = bf16[8,12,2,128,128]{4,3,2,1,0:T(8,128)(2,1)} async-done(((bf16[8,12,2,128,128]{4,3,2,1,0:T(8,128)(2,1)}), bf16[8,12,2,128,128]{4,3,2,1,0:T(8,128)(2,1)}, u32[]{:S(2)}, u32[]{:S(2)}) %all-to-all-start) | async-done | bytes 6291488 | tf_op jit(solution)/shard_map/all_to_all | solution.py:79
  288.7 4.1 %copy.55 = bf16[8,12,2,128,128]{4,3,0,2,1:T(8,128)(2,1)S(1)} copy(bf16[8,12,2,128,128]{4,3,2,1,0:T(8,128)(2,1)} %all-to-all-done) | data formatting | bytes 12582912 | tf_op jit(solution)/shard_map/all_to_all | solution.py:79
  292.9 0.4 slice_bitcast_fusion
  293.3 0.4 fusion.41
  293.7 1.0 maximum_bitcast_fusion
  294.7 0.9 copy-done.2
  295.6 5.3 %bitcast_convert_fusion = bf16[4,3,256,2,4,128]{5,2,4,3,1,0:T(8,128)(2,1)} fusion(bf16[4,3,1,2,4,256,128]{6,5,3,4,2,1,0:T(8,128)(2,1)S(1)} %get-tuple-element.24, bf16[4,3,1,2,4,256,128]{6,5,3,4,2,1,0:T(8,128)(2,1)S(1)} %get-tuple-element.23, bf16[4,3,256,2,256,1,1]{4,3,2,1,0,6,5:T(2,128)(2,1)S(1)} %bitcast.133), kind=kOutput, calls=%fused_computation.6 | convolution fusion | flops 3249537024 | bytes 22020096 | tf_op jit(solution)/shard_map/pmorajc,pmkrj->pmocak/dot_general | solution.py:88
  300.9 8.6 %copy.60 = bf16[4,3,2,128,1024]{4,3,2,1,0:T(8,128)(2,1)} copy(bf16[4,3,2,128,1024]{3,4,2,1,0:T(8,128)(2,1)} %bitcast.132) | data formatting | bytes 12582912 | tf_op jit(solution)/shard_map/convert_element_type | solution.py:91
  (25 shorter events, 0.4 us)
Async XLA Ops:
  6.5 104.2 %all-gather.2.cloned.1.call-start = ((), (), s32[]{:S(2)}) async-start(), calls=%async_computation.1 | async-start | bytes 2359296 | tf_op jit(solution)/shard_map/all_gather | solution.py:55
  7.7 1.8 copy-start.5
  103.2 4.7 %copy-start.6 = (s32[4,2]{0,1:T(2,128)S(1)}, s32[4,2]{0,1:T(2,128)}, u32[]{:S(2)}) copy-start(s32[4,2]{0,1:T(2,128)} %param.8) | copy-start | bytes 100
  103.2 4.8 %copy-start.1 = (bf16[4,1,128,4,256]{4,2,1,3,0:T(8,128)(2,1)S(1)}, bf16[4,1,128,4,256]{4,2,1,3,0:T(8,128)(2,1)}, u32[]{:S(2)}) copy-start(bf16[4,1,128,4,256]{4,2,1,3,0:T(8,128)(2,1)} %neg.44) | copy-start | bytes 3145732
  141.6 4.3 %copy-start.4 = (bf16[12,2,128,128]{3,2,1,0:T(8,128)(2,1)S(1)}, bf16[12,2,128,128]{3,2,1,0:T(8,128)(2,1)}, u32[]{:S(2)}) copy-start(bf16[12,2,128,128]{3,2,1,0:T(8,128)(2,1)} %copy.79) | copy-start | bytes 2359300
  141.6 5.3 %copy-start.3 = (bf16[12,2,128,128]{3,2,1,0:T(8,128)(2,1)S(1)}, bf16[12,2,128,128]{3,2,1,0:T(8,128)(2,1)}, u32[]{:S(2)}) copy-start(bf16[12,2,128,128]{3,2,1,0:T(8,128)(2,1)} %copy.80) | copy-start | bytes 2359300
  150.7 5.1 %copy-start = (bf16[2,3,256,512]{3,2,1,0:T(8,128)(2,1)S(1)}, bf16[2,3,256,512]{3,2,1,0:T(8,128)(2,1)}, u32[]{:S(2)}) copy-start(bf16[2,3,256,512]{3,2,1,0:T(8,128)(2,1)} %all-gather.2.cloned.1.call-done) | copy-start | bytes 4718596
  150.7 138.0 %all-to-all-start = ((bf16[8,12,2,128,128]{4,3,2,1,0:T(8,128)(2,1)}), bf16[8,12,2,128,128]{4,3,2,1,0:T(8,128)(2,1)}, u32[]{:S(2)}, u32[]{:S(2)}) async-start(bf16[8,12,2,128,128]{4,3,2,1,0:T(8,128)(2,1)} %bitcast_dynamic-update-slice_fusion), calls=%async_computation | async-start | bytes 12582912 | tf_op jit(solution)/shard_map/all_to_all | solution.py:79
  293.7 1.9 copy-start.2
Sparse Core Ops, SparseCore 0:
  96.0 7.9 all-gather.1
